TPU v7x, 32 devices: a whole 2x2x4 slice. The times are simulated.
32 devices in a mesh: rows: 4 (over y, x), cols: 8 (over z, core).
Axes of the slice: x: 2, y: 2, z: 4, core: 2. Of those that a mesh axis runs over, the one named last changes fastest.
Arguments:
- spectra: bfloat16 [1024, 4096], P(('rows', 'cols')), may hold values from -6 to 6
- band_weights: float32 [2048], replicated, may hold values from 0.3 to 3
- lag_weights: float32 [4], replicated, may hold values from 0.5 to 2
- selected_bins: int32 [8], replicated, may hold values from 0 to 7
Outputs:
- correlations: float32 [4, 1024, 1024], P(None, 'rows', 'cols')
- gradient: float32 [1024, 4096], P(('rows', 'cols'))
All inputs are finite; a program needn't handle non-finite values.
Results may differ from a plain program's by a relative error of at most 0.0045.
Values may be sent and summed in bfloat16 or wider, within the bound.
No kernel may reach another device: no remote copies, remote signals or barrier semaphores. Data moves between devices by JAX's collectives and lax.ppermute only.
A program may use at most 128 MiB of HBM per device.

v0:
```python
import jax
import jax.numpy as jnp
from jax import lax
from jax.sharding import PartitionSpec as P

LAGS = 4
LAG_STEP = 8
BIN = 128


def per_device(spectra, band_weights, lag_weights, selected_bins):
    n_rows = lax.axis_size("rows")
    n_cols = lax.axis_size("cols")
    row_index = lax.axis_index("rows")
    col_index = lax.axis_index("cols")
    freqs = band_weights.shape[0]
    raw = spectra.astype(jnp.float32)
    mean_power = jnp.mean(raw * raw, axis=1, keepdims=True)
    bin_gains = jnp.concatenate([band_weights, band_weights])
    whitened = (raw * lax.rsqrt(mean_power + 1e-05) * bin_gains[None, :]).astype(jnp.bfloat16)
    row_tile = lax.all_gather(whitened, "cols", axis=0, tiled=True)
    row_len = row_tile.shape[0]
    fold_ratio = n_cols // n_rows
    col_len = row_len // fold_ratio
    slot_part = col_index % fold_ratio
    owner_row = col_index // fold_ratio
    own_piece = lax.dynamic_slice_in_dim(row_tile, slot_part * col_len, col_len, 0)
    stacked = lax.all_gather(own_piece, "rows", axis=0, tiled=True)
    col_tile = lax.dynamic_slice_in_dim(stacked, owner_row * col_len, col_len, 0)
    row_chan = row_index * row_len + jnp.arange(row_len, dtype=jnp.int32)
    col_chan = col_index * col_len + jnp.arange(col_len, dtype=jnp.int32)
    distance = jnp.abs(row_chan[:, None] - col_chan[None, :]) // BIN
    selected = jnp.any(distance[:, :, None] == selected_bins[None, None, :], axis=2).astype(
        jnp.float32
    )
    norm_scale = 1.0 / jnp.sqrt(jnp.float32(2 * freqs))
    bin_index = jnp.arange(freqs, dtype=jnp.float32)
    real_part = row_tile[:, :freqs].astype(jnp.float32)
    imag_part = row_tile[:, freqs:].astype(jnp.float32)
    outputs = []
    row_grad = jnp.zeros((row_len, 2 * freqs), jnp.float32)
    col_grad = jnp.zeros((col_len, 2 * freqs), jnp.float32)
    for lag_index in range(LAGS):
        shift_lag = float((lag_index - LAGS // 2) * LAG_STEP)
        theta = jnp.pi * bin_index * shift_lag / freqs
        cosine = jnp.cos(theta)
        sine_part = jnp.sin(theta)
        rotated = jnp.concatenate(
            [
                real_part * cosine - imag_part * sine_part,
                imag_part * cosine + real_part * sine_part,
            ],
            axis=1,
        ).astype(jnp.bfloat16)
        correlation = (
            lax.dot_general(
                rotated, col_tile, (((1,), (1,)), ((), ())), preferred_element_type=jnp.float32
            )
            * norm_scale
        )
        outputs.append(correlation)
        adjoint = (lag_weights[lag_index] * selected * correlation).astype(jnp.bfloat16)
        back = jnp.dot(adjoint, col_tile, preferred_element_type=jnp.float32) * norm_scale
        back_real = back[:, :freqs]
        back_imag = back[:, freqs:]
        row_grad = row_grad + jnp.concatenate(
            [
                back_real * cosine + back_imag * sine_part,
                back_imag * cosine - back_real * sine_part,
            ],
            axis=1,
        )
        col_grad = (
            col_grad
            + lax.dot_general(
                adjoint, rotated, (((0,), (0,)), ((), ())), preferred_element_type=jnp.float32
            )
            * norm_scale
        )
    col_total = lax.psum(col_grad, "rows")
    is_owner = (owner_row == row_index).astype(jnp.float32)
    addition = lax.dynamic_update_slice_in_dim(
        jnp.zeros_like(row_grad), col_total * is_owner, slot_part * col_len, 0
    )
    gradient = lax.psum_scatter(row_grad + addition, "cols", scatter_dimension=0, tiled=True)
    return (jnp.stack(outputs), gradient)


def solution(mesh):
    placed = (P(("rows", "cols"), None), P(), P(), P())
    return jax.shard_map(
        per_device,
        mesh=mesh,
        in_specs=placed,
        out_specs=(P(None, "rows", "cols"), P(("rows", "cols"), None)),
        check_vma=False,
    )
```

profile of v0, /device:TPU:0, one launch (start us, length us, event | category | flops | bytes accessed | tf_op | source)
XLA Modules:
  0.0 241.0 jit_solution(7234839947374207454)
XLA Ops:
  7.2 0.0 all-gather.3.cloned.1.call-start
  7.2 0.8 pad_maximum_fusion.21
  8.0 1.1 fusion.28
  9.1 0.0 copy-start.9
  9.1 1.8 fusion.30
  10.9 0.0 all-gather.3.cloned.1.call-update
  10.9 0.0 all-gather.5.cloned.1.call-start
  11.0 32.0 %all-gather.3.cloned.1.call-done = bf16[256,4096]{1,0:T(8,128)(2,1)} async-done(((bf16[32,4096]{1,0:T(8,128)(2,1)}), bf16[256,4096]{1,0:T(8,128)(2,1)}) %all-gather.3.cloned.1.call-update) | async-done | bytes 2097168 | tf_op jit(solution)/shard_map/all_gather | solution.py:21
  43.0 2.4 %constant_dynamic-slice_fusion = bf16[128,4096]{1,0:T(8,128)(2,1)} fusion(bf16[256,4096]{1,0:T(8,128)(2,1)} %all-gather.3.cloned.1.call-done, s32[]{:T(128)S(6)} %select_n.28), kind=kLoop, calls=%fused_computation.115 | loop fusion | bytes 2097156 | tf_op jit(solution)/shard_map/dynamic_slice | solution.py:27
  45.4 0.0 all-gather.5.cloned.1.call-update
  45.5 0.0 all-reduce.2.cloned.1.call-start
  45.6 0.6 fusion.74
  46.2 0.1 fusion.42
  46.2 0.1 fusion.44
  46.3 0.1 fusion.48
  46.4 0.1 fusion.46
  46.4 0.2 add_select_fusion
  46.6 0.4 compare_reduce_fusion
  47.0 1.6 fusion.8
  48.7 3.4 %fusion.4 = (bf16[256,2048]{1,0:T(8,128)(2,1)}, bf16[256,2048]{1,0:T(8,128)(2,1)}, bf16[256,2048]{1,0:T(8,128)(2,1)}, bf16[256,2048]{1,0:T(8,128)(2,1)}, bf16[25...) fusion(f32[2048]{0:T(1024)S(1)} %get-tuple-element.30, f32[2048]{0:T(1024)S(1)} %get-tuple-element.31, ...), kind=kLoop, calls=%fused_computation.28 | loop fusion | flops 13631488 | bytes 8437760 | tf_op jit(solution)/shard_map/convert.6
  52.1 45.5 %all-gather.5.cloned.1.call-done = bf16[512,4096]{1,0:T(8,128)(2,1)} async-done(((bf16[128,4096]{1,0:T(8,128)(2,1)}), bf16[512,4096]{1,0:T(8,128)(2,1)}) %all-gather.5.cloned.1.call-update) | async-done | bytes 4194320 | tf_op jit(solution)/shard_map/all_gather | solution.py:28
  97.6 2.7 %fusion.24 = f32[256,128]{1,0:T(8,128)S(1)} fusion(bf16[256,2048]{1,0:T(8,128)(2,1)} %get-tuple-element.11, bf16[256,2048]{1,0:T(8,128)(2,1)} %get-tuple-element.10, bf16[512,4096]{1,0:T(8,128)(2,1)} %all-gather.5.cloned.1.call-done, s32[]{:T(128)S(6)} %select_n.30), kind=kOutput, calls=%fused_computation.61 | convolution fusion | flops 272662528 | bytes 3276804 | tf_op jit(solution)/shard_map/dot_general | solution.py:56
  100.3 2.7 %fusion.22 = f32[128,4096]{1,0:T(8,128)S(1)} fusion(bf16[256,2048]{1,0:T(8,128)(2,1)} %get-tuple-element.11, bf16[256,2048]{1,0:T(8,128)(2,1)} %get-tuple-element.10, f32[256,128]{1,0:T(8,128)S(1)} %fusion.24, pred[256,128]{1,0:T(8,128)(4,1)S(1)} %compare_reduce_fusion, f32[]{:T(128)} %bitcast.4), kind=kOutput, calls=%fused_computation.59 | convolution fusion | flops 272728064 | bytes 4358148 | tf_op jit(solution)/shard_map/dot_general | solution.py:75
  103.0 0.7 fusion.25
  103.8 1.3 convolution_add_fusion.2
  105.1 0.2 copy-done.7
  105.3 0.7 fusion.26
  106.0 1.3 convolution_add_fusion.1
  107.3 0.3 copy-done.5
  107.6 0.7 fusion.27
  108.3 2.5 %fusion = f32[128,4096]{1,0:T(8,128)} fusion(f32[128,4096]{1,0:T(8,128)S(1)} %convolution_add_fusion.1, bf16[256,2048]{1,0:T(8,128)(2,1)S(1)} %copy-done.4, bf16[256,2048]{1,0:T(8,128)(2,1)S(1)} %copy-done.5, f32[256,128]{1,0:T(8,128)S(1)} %fusion.27, pred[256,128]{1,0:T(8,128)(4,1)S(1)} %compare_reduce_fusion, f32[]{:T(128)} %bitcast.7), kind=kOutput, calls=%fused_computation.21 | convolution fusion | flops 273776640 | bytes 6455300 | tf_op jit(solution)/shard_map/dot_general | solution.py:75
  110.8 0.0 all-reduce.2.cloned.1.call-update
  110.9 0.2 reduce-scatter.2.cloned.1.call-start
  111.1 2.5 %convolution_multiply_fusion.3 = f32[256,4096]{1,0:T(8,128)S(1)} fusion(bf16[512,4096]{1,0:T(8,128)(2,1)} %all-gather.5.cloned.1.call-done, s32[]{:T(128)S(6)} %select_n.30, f32[256,128]{1,0:T(8,128)S(1)} %fusion.24, pred[256,128]{1,0:T(8,128)(4,1)S(1)} %compare_reduce_fusion, f32[]{:T(128)} %bitcast.4), kind=kOutput, calls=%fused_computation.19 | convolution fusion | flops 269582336 | bytes 5407236 | tf_op jit(solution)/shard_map/dot_general | solution.py:63
  113.6 0.6 multiply_add_fusion.3
  114.2 1.6 copy-done.3
  115.8 1.3 convolution_multiply_fusion.1
  117.1 0.6 multiply_add_fusion.1
  117.7 1.3 convolution_multiply_fusion
  119.1 1.3 convolution_multiply_fusion.2
  120.4 0.6 multiply_add_fusion
  121.0 0.6 multiply_add_fusion.2
  121.6 2.5 %fusion.2 = f32[256,4096]{1,0:T(8,128)} fusion(f32[256,2048]{1,0:T(8,128)S(1)} %get-tuple-element.9, f32[256,2048]{1,0:T(8,128)S(1)} %get-tuple-element.8, f32[256,2048]{1,0:T(8,128)S(1)} %get-tuple-element.7, f32[256,2048]{1,0:T(8,128)S(1)} %get-tuple-element.6, f32[256,2048]{1,0:T(8,128)S(1)} %get-tuple-element.5, f32[256,2048]{1,0:T(8,128)S(1)} %get-tuple-element.4, ...), kind=kLoop, calls=%fused_computation.26 | loop fusion | flops 7340032 | bytes 20971520 | tf_op jit(solution)/shard_map/add | solution.py:66
  124.2 56.3 %all-reduce.2.cloned.1.call-done = f32[128,4096]{1,0:T(8,128)} async-done(((f32[128,4096]{1,0:T(8,128)}), f32[128,4096]{1,0:T(8,128)}) %all-reduce.2.cloned.1.call-update) | async-done | bytes 2097168 | tf_op jit(solution)/shard_map/psum | solution.py:80
  180.5 3.8 %add_dynamic-update-slice_fusion = f32[256,4096]{1,0:T(8,128)} fusion(f32[256,4096]{1,0:T(8,128)} %fusion.2, s32[]{:T(128)S(6)} %select_n.28, f32[128,4096]{1,0:T(8,128)} %all-reduce.2.cloned.1.call-done, f32[]{:T(128)S(6)} %convert_element_type.40), kind=kLoop, calls=%fused_computation.47 | loop fusion | flops 1048576 | bytes 6291464 | tf_op jit(solution)/shard_map/add | solution.py:85
  184.3 0.0 reduce-scatter.2.cloned.1.call-update
  184.3 0.8 pad_maximum_fusion.20
  185.2 49.3 %reduce-scatter.2.cloned.1.call-done = f32[32,4096]{1,0:T(8,128)} async-done(((f32[256,4096]{1,0:T(8,128)}), f32[32,4096]{1,0:T(8,128)}) %reduce-scatter.2.cloned.1.call-update) | async-done | bytes 524304 | tf_op jit(solution)/shard_map/reduce_scatter | solution.py:85
  (19 shorter events, 0.1 us)
Async XLA Ops:
  7.2 35.8 %all-gather.3.cloned.1.call-start = ((), (), s32[]{:S(2)}) async-start(), calls=%async_computation.1 | async-start | bytes 2359296 | tf_op jit(solution)/shard_map/all_gather | solution.py:21
  8.0 37.6 %copy-start.8 = (f32[4]{0:T(128)S(1)}, f32[4]{0:T(128)}, u32[]{:S(2)}) copy-start(f32[4]{0:T(128)} %param.6) | copy-start | bytes 52
  9.1 37.5 %copy-start.9 = (s32[8]{0:T(128)S(1)}, s32[8]{0:T(128)}, u32[]{:S(2)}) copy-start(s32[8]{0:T(128)} %param.7) | copy-start | bytes 100
  10.9 86.6 %all-gather.5.cloned.1.call-start = ((), (), s32[]{:S(2)}) async-start(), calls=%async_computation.2 | async-start | bytes 5242880 | tf_op jit(solution)/shard_map/all_gather | solution.py:28
  43.0 4.0 %copy-start = (bf16[256,4096]{1,0:T(8,128)(2,1)S(1)}, bf16[256,4096]{1,0:T(8,128)(2,1)}, u32[]{:S(2)}) copy-start(bf16[256,4096]{1,0:T(8,128)(2,1)} %all-gather.3.cloned.1.call-done) | copy-start | bytes 6291460
  45.5 135.0 %all-reduce.2.cloned.1.call-start = ((), (), s32[]{:S(2)}) async-start(), calls=%async_computation.3 | async-start | bytes 4194304 | tf_op jit(solution)/shard_map/psum | solution.py:80
  97.6 5.4 %copy-start.2 = (bf16[512,4096]{1,0:T(8,128)(2,1)S(1)}, bf16[512,4096]{1,0:T(8,128)(2,1)}, u32[]{:S(2)}) copy-start(bf16[512,4096]{1,0:T(8,128)(2,1)} %all-gather.5.cloned.1.call-done) | copy-start | bytes 12582916
  100.3 2.7 %copy-start.1 = (bf16[256,2048]{1,0:T(8,128)(2,1)S(1)}, bf16[256,2048]{1,0:T(8,128)(2,1)}, u32[]{:S(2)}) copy-start(bf16[256,2048]{1,0:T(8,128)(2,1)} %get-tuple-element.13) | copy-start | bytes 3145732
  103.8 1.3 copy-start.6
  103.8 1.5 copy-start.7
  106.0 1.3 copy-start.4
  106.0 1.5 copy-start.5
  110.9 123.6 %reduce-scatter.2.cloned.1.call-start = ((), (), s32[]{:S(2)}) async-start(), calls=%async_computation.4 | async-start | bytes 4718592 | tf_op jit(solution)/shard_map/reduce_scatter | solution.py:85
  113.6 2.2 copy-start.3
Sparse Core Ops, SparseCore 0:
  11.1 31.8 all-gather.2
  45.6 51.9 all-gather.4
  111.0 69.4 all-reduce.1
  184.5 49.9 reduce-scatter.1
where the time goes:
time: 241 us
  waiting for transfers between devices  183 us (76%)
  matrix products  19.2 us (8%)
  other arithmetic  19.1 us (8%)
  between operations  14.1 us (6%)
  local copies, waits for them, and re-layouts  5.18 us (2%)
    psum x1, waiting for transfers between devices, per_device(): col_total = lax.psum(col_grad, 'rows')  56.3 us
    reduce_scatter x1, waiting for transfers between devices, per_device(): lax.psum_scatter(row_grad + addition, 'cols', scatter_dimension=0, tiled=...  49.3 us
    all_gather x1, waiting for transfers between devices, per_device(): stacked = lax.all_gather(own_piece, 'rows', axis=0, tiled=True)  45.5 us
    all_gather x1, waiting for transfers between devices, per_device(): row_tile = lax.all_gather(whitened, 'cols', axis=0, tiled=True)  32 us
    dot_general x4, matrix products, per_device(): lax.dot_general(adjoint, rotated, (((0,), (0,)), ((), ())), preferred_ele...  7.8 us
    dot_general x4, matrix products, per_device(): jnp.dot(adjoint, col_tile, preferred_element_type=jnp.float32) * norm_scale  6.53 us
    another operation x2, other arithmetic  5.08 us
    dot_general x4, matrix products, per_device(): lax.dot_general(rotated, col_tile, (((1,), (1,)), ((), ())), preferred_el...  4.84 us
  transfers between devices with their start and end apart: 4, of which 4 were waited for; matrix products, arithmetic and copies ran while one was open for 8% of the time, Pallas kernels for 0%

commit v1 on v0

--- a/solution.py
+++ b/solution.py
@@ -6,6 +6,15 @@
 LAGS = 4
 LAG_STEP = 8
 BIN = 128
+
+
+def add_in_pairs(x, name):
+    devices = lax.axis_size(name)
+    total, reach = (x, 1)
+    while reach < devices:
+        total = total + lax.ppermute(total, name, [(i, i ^ reach) for i in range(devices)])
+        reach = 2 * reach
+    return total
 
 
 def per_device(spectra, band_weights, lag_weights, selected_bins):
@@ -77,7 +86,7 @@
             )
             * norm_scale
         )
-    col_total = lax.psum(col_grad, "rows")
+    col_total = add_in_pairs(col_grad, "rows")
     is_owner = (owner_row == row_index).astype(jnp.float32)
     addition = lax.dynamic_update_slice_in_dim(
         jnp.zeros_like(row_grad), col_total * is_owner, slot_part * col_len, 0

time: 241 us -> 264 us (1.095)
  waiting for transfers between devices: 183 us -> 206 us
  starting transfers between devices: 0.35 us -> 3.18 us
    ppermute x0 -> x2, waiting for transfers between devices: none -> 79.6 us  [add_in_pairs(): lax.ppermute(total, name, [(i, i ^ reach) for i in range(devices)])]
    psum x1 -> x0, waiting for transfers between devices: 56.3 us -> none  [per_device(): col_total = lax.psum(col_grad, 'rows')]
    ppermute x0 -> x2, starting transfers between devices: none -> 3.05 us  [add_in_pairs(): lax.ppermute(total, name, [(i, i ^ reach) for i in range(devices)])]
  transfers between devices with their start and end apart: 4 -> 5, of which waited for: 4 -> 5; matrix products, arithmetic and copies ran while one was open for 8% -> 7% of each run, Pallas kernels for 0% -> 0%
where the time goes in v1:
time: 264 us; the launch traced here: 263 us
  waiting for transfers between devices  206 us (78%)
  other arithmetic  19.6 us (7%)
  matrix products  16.7 us (6%)
  between operations  14.1 us (5%)
  local copies, waits for them, and re-layouts  3.54 us (1%)
  starting transfers between devices  3.18 us (1%)
    ppermute x2, waiting for transfers between devices, add_in_pairs(): lax.ppermute(total, name, [(i, i ^ reach) for i in range(devices)])  79.6 us
    reduce_scatter x1, waiting for transfers between devices, per_device(): lax.psum_scatter(row_grad + addition, 'cols', scatter_dimension=0, tiled=...  49.2 us
    all_gather x1, waiting for transfers between devices, per_device(): stacked = lax.all_gather(own_piece, 'rows', axis=0, tiled=True)  45.5 us
    all_gather x1, waiting for transfers between devices, per_device(): row_tile = lax.all_gather(whitened, 'cols', axis=0, tiled=True)  32 us
    dot_general x4, matrix products, per_device(): lax.dot_general(adjoint, rotated, (((0,), (0,)), ((), ())), preferred_ele...  6.51 us
    dot_general x4, matrix products, per_device(): jnp.dot(adjoint, col_tile, preferred_element_type=jnp.float32) * norm_scale  5.35 us
  transfers between devices with their start and end apart: 5, of which 5 were waited for; matrix products, arithmetic and copies ran while one was open for 7% of the time, Pallas kernels for 0%

profile of v1, /device:TPU:0, one launch (start us, length us, event | category | flops | bytes accessed | tf_op | source)
XLA Modules:
  0.0 263.3 jit_solution(4525904763638092327)
XLA Ops:
  7.2 0.0 all-gather.3.cloned.1.call-start
  7.2 0.8 pad_maximum_fusion.21
  8.0 1.1 fusion.28
  9.1 1.8 fusion.30
  10.9 0.0 all-gather.3.cloned.1.call-update
  10.9 0.0 all-gather.5.cloned.1.call-start
  11.0 32.0 %all-gather.3.cloned.1.call-done = bf16[256,4096]{1,0:T(8,128)(2,1)} async-done(((bf16[32,4096]{1,0:T(8,128)(2,1)}), bf16[256,4096]{1,0:T(8,128)(2,1)}) %all-gather.3.cloned.1.call-update) | async-done | bytes 2097168 | tf_op jit(solution)/shard_map/all_gather | solution.py:30
  43.0 2.4 constant_dynamic-slice_fusion
  45.4 0.0 all-gather.5.cloned.1.call-update
  45.4 0.0 reduce-scatter.2.cloned.1.call-start
  45.6 0.7 fusion.74
  46.2 0.1 fusion.42
  46.3 0.1 fusion.44
  46.3 0.1 fusion.48
  46.4 0.1 fusion.46
  46.4 0.2 add_select_fusion
  46.6 0.4 compare_reduce_fusion
  47.0 1.7 fusion.8
  48.7 3.4 %fusion.4 = (bf16[256,2048]{1,0:T(8,128)(2,1)}, bf16[256,2048]{1,0:T(8,128)(2,1)}, bf16[256,2048]{1,0:T(8,128)(2,1)}, bf16[256,2048]{1,0:T(8,128)(2,1)}, bf16[25...) fusion(f32[2048]{0:T(1024)S(1)} %get-tuple-element.30, f32[2048]{0:T(1024)S(1)} %get-tuple-element.31, ...), kind=kLoop, calls=%fused_computation.28 | loop fusion | flops 13631488 | bytes 8437760 | tf_op jit(solution)/shard_map/convert.6
  52.1 45.5 %all-gather.5.cloned.1.call-done = bf16[512,4096]{1,0:T(8,128)(2,1)} async-done(((bf16[128,4096]{1,0:T(8,128)(2,1)}), bf16[512,4096]{1,0:T(8,128)(2,1)}) %all-gather.5.cloned.1.call-update) | async-done | bytes 4194320 | tf_op jit(solution)/shard_map/all_gather | solution.py:37
  97.6 2.7 %fusion.24 = f32[256,128]{1,0:T(8,128)S(1)} fusion(bf16[256,2048]{1,0:T(8,128)(2,1)} %get-tuple-element.11, bf16[256,2048]{1,0:T(8,128)(2,1)} %get-tuple-element.10, bf16[512,4096]{1,0:T(8,128)(2,1)} %all-gather.5.cloned.1.call-done, s32[]{:T(128)S(6)} %select_n.30), kind=kOutput, calls=%fused_computation.61 | convolution fusion | flops 272662528 | bytes 3276804 | tf_op jit(solution)/shard_map/dot_general | solution.py:65
  100.3 2.7 %fusion.22 = f32[128,4096]{1,0:T(8,128)S(1)} fusion(bf16[256,2048]{1,0:T(8,128)(2,1)} %get-tuple-element.11, bf16[256,2048]{1,0:T(8,128)(2,1)} %get-tuple-element.10, f32[256,128]{1,0:T(8,128)S(1)} %fusion.24, pred[256,128]{1,0:T(8,128)(4,1)S(1)} %compare_reduce_fusion, f32[]{:T(128)} %bitcast.4), kind=kOutput, calls=%fused_computation.59 | convolution fusion | flops 272728064 | bytes 4358148 | tf_op jit(solution)/shard_map/dot_general | solution.py:84
  103.0 0.7 fusion.25
  103.8 1.3 convolution_add_fusion.2
  105.1 0.2 copy-done.6
  105.3 0.7 fusion.26
  106.0 1.3 convolution_add_fusion.1
  107.4 0.2 copy-done.4
  107.6 0.7 fusion.27
  108.3 1.2 fusion
  109.5 1.5 collective-permute-start
  111.0 1.3 convolution_multiply_fusion.3
  112.3 1.4 convolution_multiply_fusion.1
  113.7 1.3 convolution_multiply_fusion
  115.0 0.8 multiply_add_fusion.3
  115.9 0.9 multiply_add_fusion.1
  116.8 40.0 %collective-permute-done = f32[128,4096]{1,0:T(8,128)S(1)} collective-permute-done((f32[128,4096]{1,0:T(8,128)S(1)}, f32[128,4096]{1,0:T(8,128)S(1)}, u32[]{:S(2)}, u32[]{:S(2)}) %collective-permute-start) | collective-permute-done | bytes 2097184 | tf_op jit(solution)/shard_map/ppermute | solution.py:15
  156.8 0.2 add.131
  157.0 1.5 collective-permute-start.1
  158.5 1.3 convolution_multiply_fusion.2
  159.9 0.6 multiply_add_fusion
  160.5 0.8 multiply_add_fusion.2
  161.3 2.5 fusion.2
  163.8 39.6 %collective-permute-done.1 = f32[128,4096]{1,0:T(8,128)S(1)} collective-permute-done((f32[128,4096]{1,0:T(8,128)S(1)}, f32[128,4096]{1,0:T(8,128)S(1)}, u32[]{:S(2)}, u32[]{:S(2)}) %collective-permute-start.1) | collective-permute-done | bytes 2097184 | tf_op jit(solution)/shard_map/ppermute | solution.py:15
  203.4 3.3 %add_dynamic-update-slice_fusion = f32[256,4096]{1,0:T(8,128)} fusion(f32[256,4096]{1,0:T(8,128)} %fusion.2, s32[]{:T(128)S(6)} %select_n.28, f32[128,4096]{1,0:T(8,128)S(1)} %add.131, f32[128,4096]{1,0:T(8,128)S(1)} %collective-permute-done.1, f32[]{:T(128)S(6)} %convert_element_type.40), kind=kLoop, calls=%fused_computation.47 | loop fusion | flops 1572864 | bytes 8388616 | tf_op jit(solution)/shard_map/add | solution.py:94
  206.7 0.0 reduce-scatter.2.cloned.1.call-update
  206.8 0.8 pad_maximum_fusion.20
  207.6 49.2 %reduce-scatter.2.cloned.1.call-done = f32[32,4096]{1,0:T(8,128)} async-done(((f32[256,4096]{1,0:T(8,128)}), f32[32,4096]{1,0:T(8,128)}) %reduce-scatter.2.cloned.1.call-update) | async-done | bytes 524304 | tf_op jit(solution)/shard_map/reduce_scatter | solution.py:94
  (19 shorter events, 0.1 us)
Async XLA Ops:
  7.2 35.8 %all-gather.3.cloned.1.call-start = ((), (), s32[]{:S(2)}) async-start(), calls=%async_computation.1 | async-start | bytes 2359296 | tf_op jit(solution)/shard_map/all_gather | solution.py:30
  8.0 37.6 %copy-start.7 = (f32[4]{0:T(128)S(1)}, f32[4]{0:T(128)}, u32[]{:S(2)}) copy-start(f32[4]{0:T(128)} %param.6) | copy-start | bytes 52
  9.1 37.5 %copy-start.8 = (s32[8]{0:T(128)S(1)}, s32[8]{0:T(128)}, u32[]{:S(2)}) copy-start(s32[8]{0:T(128)} %param.7) | copy-start | bytes 100
  10.9 86.6 %all-gather.5.cloned.1.call-start = ((), (), s32[]{:S(2)}) async-start(), calls=%async_computation.2 | async-start | bytes 5242880 | tf_op jit(solution)/shard_map/all_gather | solution.py:37
  43.0 4.1 %copy-start = (bf16[256,4096]{1,0:T(8,128)(2,1)S(1)}, bf16[256,4096]{1,0:T(8,128)(2,1)}, u32[]{:S(2)}) copy-start(bf16[256,4096]{1,0:T(8,128)(2,1)} %all-gather.3.cloned.1.call-done) | copy-start | bytes 6291460
  45.4 211.4 %reduce-scatter.2.cloned.1.call-start = ((), (), s32[]{:S(2)}) async-start(), calls=%async_computation.3 | async-start | bytes 4718592 | tf_op jit(solution)/shard_map/reduce_scatter | solution.py:94
  97.6 5.4 %copy-start.2 = (bf16[512,4096]{1,0:T(8,128)(2,1)S(1)}, bf16[512,4096]{1,0:T(8,128)(2,1)}, u32[]{:S(2)}) copy-start(bf16[512,4096]{1,0:T(8,128)(2,1)} %all-gather.5.cloned.1.call-done) | copy-start | bytes 12582916
  100.3 2.7 %copy-start.1 = (bf16[256,2048]{1,0:T(8,128)(2,1)S(1)}, bf16[256,2048]{1,0:T(8,128)(2,1)}, u32[]{:S(2)}) copy-start(bf16[256,2048]{1,0:T(8,128)(2,1)} %get-tuple-element.13) | copy-start | bytes 3145732
  103.8 1.3 copy-start.5
  103.8 1.5 copy-start.6
  106.0 1.4 copy-start.3
  106.0 1.5 copy-start.4
  109.5 47.3 %collective-permute-start = (f32[128,4096]{1,0:T(8,128)S(1)}, f32[128,4096]{1,0:T(8,128)S(1)}, u32[]{:S(2)}, u32[]{:S(2)}) collective-permute-start(f32[128,4096]{1,0:T(8,128)S(1)} %fusion), channel_id=1, source_target_pairs={{0,8},{8,0},{16,24},{24,16},{1,9},{9,1},{17,25},{25,17},{2,10},{10... | collective-permute-start | bytes 6291464 | tf_op jit(solution)/shard_map/ppermute | solution.py:15
  157.0 46.4 %collective-permute-start.1 = (f32[128,4096]{1,0:T(8,128)S(1)}, f32[128,4096]{1,0:T(8,128)S(1)}, u32[]{:S(2)}, u32[]{:S(2)}) collective-permute-start(f32[128,4096]{1,0:T(8,128)S(1)} %add.131), channel_id=1, source_target_pairs={{0,16},{8,24},{16,0},{24,8},{1,17},{9,25},{17,1},{25,9},{2,18},{10... | collective-permute-start | bytes 6291464 | tf_op jit(solution)/shard_map/ppermute | solution.py:15
Sparse Core Ops, SparseCore 0:
  11.1 31.8 all-gather.2
  45.6 51.9 all-gather.4
  206.9 49.8 reduce-scatter.1
